TPU v7x, 128 devices: a whole 4x4x4 slice. The times are simulated.
128 devices in a mesh: dp: 4 (over x_hi, core), expert: 32 (over z, y, x_lo).
Axes of the slice: x: 4 (x_hi: 2, x_lo: 2; x = x_hi * 2 + x_lo), y: 4, z: 4, core: 2. Of those that a mesh axis runs over, the one named last changes fastest.
Arguments:
- tokens: bfloat16 [16384, 3072], P(('dp', 'expert')), may hold values from -6 to 6
- target: bfloat16 [16384, 3072], P(('dp', 'expert')), may hold values from -3 to 3
- routes: int32 [16384, 1], P(('dp', 'expert')), may hold values from 0 to 31; in each aligned block of 128 rows (0 to 127, 128 to 255, ...) at most 6 rows name the same one
- thresholds: int32 [32, 2048], P('expert', 'dp'), may hold values from 0 to 3
- enc_weight: bfloat16 [32, 3072, 2048], P('expert', None, 'dp'), may hold values from -0.109375 to 0.109375
- dec_weight: bfloat16 [32, 3072, 2048], P('expert', None, 'dp'), may hold values from -0.125 to 0.125
Outputs:
- recon: bfloat16 [16384, 3072], P(('dp', 'expert'))
- grad_enc: bfloat16 [32, 3072, 2048], P('expert', None, 'dp')
- grad_dec: bfloat16 [32, 3072, 2048], P('expert', None, 'dp')
Inputs may be any that keep to these rules, and one draw needn't show every extreme that they name: `routes`: within the rows of one device no expert is named by more than 6 rows, a bound that some block reaches.
All inputs are finite; a program needn't handle non-finite values.
Results may differ from a plain program's by a relative error of at most 0.012.
Values may be sent and summed in bfloat16 or wider, within the bound.
A program may use at most 128 MiB of HBM per device.

v0:
```python
import jax
import jax.numpy as jnp
from jax import lax
from jax.sharding import PartitionSpec as P

error_scale = 0.03125


def slot_table(route_col, experts, capacity):
    choices = route_col[:, 0]
    one_hot = (choices[:, None] == jnp.arange(experts, dtype=jnp.int32)[None, :]).astype(jnp.int32)
    ranking = jnp.sum((jnp.cumsum(one_hot, axis=0) - 1) * one_hot, axis=1)
    slot_idx = choices * capacity + ranking
    positions = jnp.arange(experts * capacity, dtype=jnp.int32)
    return (positions[:, None] == slot_idx[None, :]).astype(jnp.bfloat16)


def local(tokens, target, routes, thresholds, enc_weight, dec_weight):
    experts = lax.axis_size("expert")
    per_dev = tokens.shape[0]
    features = tokens.shape[1]
    capacity = 3 * per_dev // (2 * experts)
    placing = slot_table(routes, experts, capacity)
    outbox = (
        jnp.dot(placing, tokens, preferred_element_type=jnp.float32)
        .astype(jnp.bfloat16)
        .reshape(experts, capacity, features)
    )
    column_rows = lax.all_gather(outbox[:, None], "dp", axis=1, tiled=True)
    arrived = lax.all_to_all(column_rows, "expert", split_axis=0, concat_axis=0, tiled=True)
    row_axis = 1
    leading = arrived.shape[:2]
    arrived_rows = arrived.reshape(-1, features)
    enc_part = enc_weight[0]
    dec_part = dec_weight[0]
    shifts = 0.25 * thresholds[0].astype(jnp.float32)
    latent_pre = jnp.dot(arrived_rows, enc_part, preferred_element_type=jnp.float32) - shifts
    squash = jax.nn.sigmoid(4.0 * latent_pre)
    activity = (latent_pre * squash).astype(jnp.bfloat16)
    derivative = squash + 4.0 * latent_pre * squash * (1.0 - squash)
    partials = lax.dot_general(
        activity, dec_part, (((1,), (1,)), ((), ())), preferred_element_type=jnp.float32
    )
    own_sums = lax.psum_scatter(
        partials.reshape(leading + (capacity, features)).astype(jnp.bfloat16),
        "dp",
        scatter_dimension=row_axis,
        tiled=True,
    )
    recon_rows = own_sums.reshape(experts, capacity, features)
    returned = lax.all_to_all(recon_rows, "expert", split_axis=0, concat_axis=0, tiled=True)
    recon = lax.dot_general(
        placing,
        returned.reshape(-1, features),
        (((0,), (0,)), ((), ())),
        preferred_element_type=jnp.float32,
    ).astype(jnp.bfloat16)
    error_tok = ((recon.astype(jnp.float32) - target.astype(jnp.float32)) * error_scale).astype(
        jnp.bfloat16
    )
    error_box = (
        jnp.dot(placing, error_tok, preferred_element_type=jnp.float32)
        .astype(jnp.bfloat16)
        .reshape(experts, capacity, features)
    )
    column_errors = lax.all_gather(error_box[:, None], "dp", axis=1, tiled=True)
    error_in = lax.all_to_all(column_errors, "expert", split_axis=0, concat_axis=0, tiled=True)
    error_rows = error_in.reshape(-1, features)
    grad_dec = lax.dot_general(
        error_rows, activity, (((0,), (0,)), ((), ())), preferred_element_type=jnp.float32
    ).astype(jnp.bfloat16)
    grad_act = jnp.dot(error_rows, dec_part, preferred_element_type=jnp.float32)
    grad_pre = (grad_act * derivative).astype(jnp.bfloat16)
    grad_enc = lax.dot_general(
        arrived_rows, grad_pre, (((0,), (0,)), ((), ())), preferred_element_type=jnp.float32
    ).astype(jnp.bfloat16)
    return (recon, grad_enc[None], grad_dec[None])


def solution(mesh):
    in_specs = (
        P(("dp", "expert"), None),
        P(("dp", "expert"), None),
        P(("dp", "expert"), None),
        P("expert", "dp"),
        P("expert", None, "dp"),
        P("expert", None, "dp"),
    )
    out_specs = (P(("dp", "expert"), None), P("expert", None, "dp"), P("expert", None, "dp"))
    return jax.shard_map(local, mesh=mesh, in_specs=in_specs, out_specs=out_specs, check_vma=False)
```

profile of v0, /device:TPU:1, one launch (start us, length us, event | category | flops | bytes accessed | tf_op | source)
XLA Modules:
  0.0 423.9 jit_solution(15606103970042504576)
XLA Ops:
  7.2 0.0 copy-start
  7.2 0.0 all-gather.3.cloned.1.call-start
  7.2 0.9 fusion.11
  8.1 0.2 reduce_window_sum.11
  8.3 0.8 select_reduce_fusion
  9.1 0.7 multiply_add_fusion
  9.8 2.6 convolution_convert_fusion.4
  12.4 2.4 broadcast_in_dim_reshape.6
  14.8 3.1 copy.14
  17.9 0.0 all-gather.3.cloned.1.call-update
  17.9 45.2 %all-gather.3.cloned.1.call-done = bf16[32,4,6,3072]{3,0,2,1:T(8,128)(2,1)} async-done(((bf16[32,1,6,3072]{3,0,2,1:T(8,128)(2,1)}), bf16[32,4,6,3072]{3,0,2,1:T(8,128)(2,1)}) %all-gather.3.cloned.1.call-update) | async-done | bytes 4718608 | tf_op jit(solution)/shard_map/all_gather | solution.py:29
  63.1 8.1 %copy.15 = bf16[32,4,6,3072]{3,1,2,0:T(4,128)(2,1)} copy(bf16[32,4,6,3072]{3,0,2,1:T(8,128)(2,1)} %all-gather.3.cloned.1.call-done) | data formatting | bytes 9437184 | tf_op jit(solution)/shard_map/all_gather | solution.py:29
  71.2 0.0 copy-start.3
  71.2 7.2 %all-to-all-start = ((bf16[32,4,6,3072]{3,1,2,0:T(4,128)(2,1)}), bf16[32,4,6,3072]{3,1,2,0:T(4,128)(2,1)}, u32[]{:S(2)}, u32[]{:S(2)}) async-start(bf16[32,4,6,3072]{3,1,2,0:T(4,128)(2,1)} %copy.15), calls=%async_computation | async-start | bytes 9437184 | tf_op jit(solution)/shard_map/all_to_all | solution.py:30
  78.5 0.2 reduce-scatter.2.cloned.1.call-start
  78.7 0.0 copy-done.3
  78.7 63.8 %all-to-all-done = bf16[32,4,6,3072]{3,1,2,0:T(4,128)(2,1)} async-done(((bf16[32,4,6,3072]{3,1,2,0:T(4,128)(2,1)}), bf16[32,4,6,3072]{3,1,2,0:T(4,128)(2,1)}, u32[]{:S(2)}, u32[]{:S(2)}) %all-to-all-start) | async-done | bytes 4718624 | tf_op jit(solution)/shard_map/all_to_all | solution.py:30
  142.5 7.1 %copy.16 = bf16[32,4,6,3072]{3,2,1,0:T(8,128)(2,1)} copy(bf16[32,4,6,3072]{3,1,2,0:T(4,128)(2,1)} %all-to-all-done) | data formatting | bytes 9437184 | tf_op jit(solution)/shard_map/all_to_all | solution.py:30
  149.6 7.8 %reshape.28 = bf16[768,3072]{1,0:T(8,128)(2,1)} reshape(bf16[32,4,6,3072]{3,2,1,0:T(8,128)(2,1)} %copy.16) | data formatting | bytes 9437184 | tf_op jit(solution)/shard_map/reshape | solution.py:33
  157.5 7.5 %multiply_convert_fusion.2 = (bf16[768,512]{1,0:T(8,128)(2,1)}, f32[768,512]{1,0:T(8,128)}) fusion(f32[512]{0:T(512)S(1)} %bitcast.43, bf16[768,3072]{1,0:T(8,128)(2,1)} %reshape.28, bf16[1,3072,512]{2,1,0:T(8,128)(2,1)} %param.10), kind=kOutput, calls=%fused_computation.15 | convolution fusion | flops 2418671616 | bytes 10225664 | tf_op jit(solution)/shard_map/dot_general | solution.py:37
  164.9 2.1 dot_general.28
  167.1 0.0 copy-done
  167.1 5.8 %convolution_convert_fusion = bf16[32,4,6,3072]{3,0,2,1:T(8,128)(2,1)} fusion(bf16[1,3072,512]{2,1,0:T(8,128)(2,1)S(1)} %copy-done, bf16[32,4,6,512]{3,2,1,0:T(8,128)(2,1)} %dot_general.28), kind=kOutput, calls=%fused_computation | convolution fusion | flops 2418278400 | bytes 8650752 | tf_op jit(solution)/shard_map/dot_general | solution.py:41
  172.9 0.0 reduce-scatter.2.cloned.1.call-update
  172.9 0.0 all-gather.5.cloned.1.call-start
  172.9 61.2 %reduce-scatter.2.cloned.1.call-done = bf16[32,1,6,3072]{3,0,2,1:T(8,128)(2,1)} async-done(((bf16[32,4,6,3072]{3,0,2,1:T(8,128)(2,1)}), bf16[32,1,6,3072]{3,0,2,1:T(8,128)(2,1)}) %reduce-scatter.2.cloned.1.call-update) | async-done | bytes 1179664 | tf_op jit(solution)/shard_map/reduce_scatter | solution.py:44
  234.1 1.9 copy.18
  236.1 29.2 %all_to_all.15 = bf16[32,6,3072]{2,1,0:T(8,128)(2,1)} all-to-all(bf16[32,6,3072]{2,1,0:T(8,128)(2,1)S(1)} %copy.18), channel_id=1, replica_groups=mesh['dp'=4,'expert'=32] {'expert'}, dimensions={0} | all-to-all | bytes 2359296 | tf_op jit(solution)/shard_map/all_to_all | solution.py:51
  265.2 2.4 reshape.30
  267.6 0.0 copy-start.2
  267.6 1.8 convolution_convert_fusion.5
  269.4 0.0 copy-start.1
  269.4 0.9 copy-done.1
  270.3 0.0 copy-done.2
  270.3 1.5 convolution_convert_fusion.3
  271.8 2.4 broadcast_in_dim_reshape.7
  274.2 3.1 copy.19
  277.3 0.0 all-gather.5.cloned.1.call-update
  277.3 40.2 %all-gather.5.cloned.1.call-done = bf16[32,4,6,3072]{3,0,2,1:T(8,128)(2,1)} async-done(((bf16[32,1,6,3072]{3,0,2,1:T(8,128)(2,1)}), bf16[32,4,6,3072]{3,0,2,1:T(8,128)(2,1)}) %all-gather.5.cloned.1.call-update) | async-done | bytes 4718608 | tf_op jit(solution)/shard_map/all_gather | solution.py:66
  317.4 6.0 %copy.20 = bf16[32,4,6,3072]{3,1,2,0:T(4,128)(2,1)S(1)} copy(bf16[32,4,6,3072]{3,0,2,1:T(8,128)(2,1)} %all-gather.5.cloned.1.call-done) | data formatting | bytes 9437184 | tf_op jit(solution)/shard_map/all_gather | solution.py:66
  323.4 63.2 %all_to_all.16 = bf16[32,4,6,3072]{3,1,2,0:T(4,128)(2,1)S(1)} all-to-all(bf16[32,4,6,3072]{3,1,2,0:T(4,128)(2,1)S(1)} %copy.20), channel_id=1, replica_groups=mesh['dp'=4,'expert'=32] {'expert'}, dimensions={0} | all-to-all | bytes 9437184 | tf_op jit(solution)/shard_map/all_to_all | solution.py:67
  386.6 4.8 %copy.21 = bf16[32,4,6,3072]{3,2,1,0:T(8,128)(2,1)} copy(bf16[32,4,6,3072]{3,1,2,0:T(4,128)(2,1)S(1)} %all_to_all.16) | data formatting | bytes 9437184 | tf_op jit(solution)/shard_map/all_to_all | solution.py:67
  391.4 7.7 %reshape.31 = bf16[768,3072]{1,0:T(8,128)(2,1)} reshape(bf16[32,4,6,3072]{3,2,1,0:T(8,128)(2,1)} %copy.21) | data formatting | bytes 9437184 | tf_op jit(solution)/shard_map/reshape | solution.py:68
  399.1 6.9 %fusion.1 = bf16[1,3072,512]{2,1,0:T(8,128)(2,1)} fusion(bf16[768,3072]{1,0:T(8,128)(2,1)} %reshape.31, bf16[768,512]{1,0:T(8,128)(2,1)} %get-tuple-element.3), kind=kOutput, calls=%fused_computation.4 | convolution fusion | flops 2417491968 | bytes 8650752 | tf_op jit(solution)/shard_map/dot_general | solution.py:69
  406.0 11.3 %fusion = bf16[1,3072,512]{2,1,0:T(8,128)(2,1)} fusion(bf16[768,3072]{1,0:T(8,128)(2,1)} %reshape.28, bf16[768,3072]{1,0:T(8,128)(2,1)} %reshape.31, bf16[1,3072,512]{2,1,0:T(8,128)(2,1)S(1)} %copy-done, f32[768,512]{1,0:T(8,128)} %get-tuple-element.4, f32[512]{0:T(512)S(1)} %bitcast.44), kind=kOutput, calls=%fused_computation.3 | convolution fusion | flops 4837736448 | bytes 17303552 | tf_op jit(solution)/shard_map/dot_general | solution.py:74
  (1 shorter events, 0.0 us)
Async XLA Ops:
  7.2 159.9 %copy-start = (bf16[1,3072,512]{2,1,0:T(8,128)(2,1)S(1)}, bf16[1,3072,512]{2,1,0:T(8,128)(2,1)}, u32[]{:S(2)}) copy-start(bf16[1,3072,512]{2,1,0:T(8,128)(2,1)} %param.11) | copy-start | bytes 9437188
  7.2 55.9 %all-gather.3.cloned.1.call-start = ((), (), s32[]{:S(2)}) async-start(), calls=%async_computation.4 | async-start | bytes 5898240 | tf_op jit(solution)/shard_map/all_gather | solution.py:29
  71.2 7.5 %copy-start.3 = (s32[1,512]{1,0:T(1,128)S(1)}, s32[1,512]{1,0:T(1,128)}, u32[]{:S(2)}) copy-start(s32[1,512]{1,0:T(1,128)} %param.9) | copy-start | bytes 6148
  71.2 71.3 %all-to-all-start = ((bf16[32,4,6,3072]{3,1,2,0:T(4,128)(2,1)}), bf16[32,4,6,3072]{3,1,2,0:T(4,128)(2,1)}, u32[]{:S(2)}, u32[]{:S(2)}) async-start(bf16[32,4,6,3072]{3,1,2,0:T(4,128)(2,1)} %copy.15), calls=%async_computation | async-start | bytes 9437184 | tf_op jit(solution)/shard_map/all_to_all | solution.py:30
  78.5 155.7 %reduce-scatter.2.cloned.1.call-start = ((), (), s32[]{:S(2)}) async-start(), calls=%async_computation.5 | async-start | bytes 5898240 | tf_op jit(solution)/shard_map/reduce_scatter | solution.py:44
  172.9 144.6 %all-gather.5.cloned.1.call-start = ((), (), s32[]{:S(2)}) async-start(), calls=%async_computation.6 | async-start | bytes 5898240 | tf_op jit(solution)/shard_map/all_gather | solution.py:66
  267.6 2.7 copy-start.2
  269.4 0.9 copy-start.1
Sparse Core Ops, SparseCore 0:
  18.0 45.0 all-gather.2
  173.0 61.0 reduce-scatter.1
  277.4 39.9 all-gather.4
where the time goes:
time: 425 us; the launch traced here: 424 us
  waiting for transfers between devices  210 us (49%)
  blocking collectives  92.4 us (22%)
  local copies, waits for them, and re-layouts  59.8 us (14%)
  matrix products  37.3 us (9%)
  between operations  13.8 us (3%)
  starting transfers between devices  7.54 us (2%)
    all_to_all x1, waiting for transfers between devices, local(): lax.all_to_all(column_rows, 'expert', split_axis=0, concat_axis=0, tiled=...  63.8 us
    all_to_all x1, blocking collectives, local(): lax.all_to_all(column_errors, 'expert', split_axis=0, concat_axis=0, tile...  63.2 us
    reduce_scatter x1, waiting for transfers between devices, local(): lax.psum_scatter(partials.reshape(leading + (capacity, features)).astype(...  61.2 us
    all_gather x1, waiting for transfers between devices, local(): column_rows = lax.all_gather(outbox[:, None], 'dp', axis=1, tiled=True)  45.2 us
    all_gather x1, waiting for transfers between devices, local(): column_errors = lax.all_gather(error_box[:, None], 'dp', axis=1, tiled=True)  40.2 us
    all_to_all x1, blocking collectives, local(): lax.all_to_all(recon_rows, 'expert', split_axis=0, concat_axis=0, tiled=T...  29.2 us
    dot_general x1, matrix products, local(): lax.dot_general(arrived_rows, grad_pre, (((0,), (0,)), ((), ())), preferr...  11.3 us
  transfers between devices with their start and end apart: 4, of which 4 were waited for; matrix products, arithmetic and copies ran while one was open for 0% of the time, Pallas kernels for 0%

commit v1 on v0

--- a/solution.py
+++ b/solution.py
@@ -4,6 +4,7 @@
 from jax.sharding import PartitionSpec as P
 
 error_scale = 0.03125
+vacant_mark = 512.0
 
 
 def slot_table(route_col, experts, capacity):
@@ -21,16 +22,18 @@
     features = tokens.shape[1]
     capacity = 3 * per_dev // (2 * experts)
     placing = slot_table(routes, experts, capacity)
-    outbox = (
-        jnp.dot(placing, tokens, preferred_element_type=jnp.float32)
-        .astype(jnp.bfloat16)
-        .reshape(experts, capacity, features)
-    )
-    column_rows = lax.all_gather(outbox[:, None], "dp", axis=1, tiled=True)
-    arrived = lax.all_to_all(column_rows, "expert", split_axis=0, concat_axis=0, tiled=True)
-    row_axis = 1
-    leading = arrived.shape[:2]
-    arrived_rows = arrived.reshape(-1, features)
+    vacant = 1.0 - jnp.sum(placing.astype(jnp.float32), axis=1, keepdims=True)
+    outbox = jnp.dot(placing, tokens, preferred_element_type=jnp.float32).astype(jnp.bfloat16)
+    target_box = (
+        jnp.dot(placing, target, preferred_element_type=jnp.float32) + vacant * vacant_mark
+    ).astype(jnp.bfloat16)
+    arrived = lax.all_to_all(
+        outbox.reshape(experts, capacity, features), "expert", split_axis=0, concat_axis=0, tiled=True
+    ).reshape(-1, features)
+    target_rows = lax.all_to_all(
+        target_box.reshape(experts, capacity, features), "expert", split_axis=0, concat_axis=0, tiled=True
+    ).reshape(-1, features)
+    arrived_rows = lax.all_gather(arrived, "dp", axis=0, tiled=True)
     enc_part = enc_weight[0]
     dec_part = dec_weight[0]
     shifts = 0.25 * thresholds[0].astype(jnp.float32)
@@ -40,32 +43,20 @@
     derivative = squash + 4.0 * latent_pre * squash * (1.0 - squash)
     partials = lax.dot_general(
         activity, dec_part, (((1,), (1,)), ((), ())), preferred_element_type=jnp.float32
+    ).astype(jnp.bfloat16)
+    recon_rows = lax.psum_scatter(partials, "dp", scatter_dimension=0, tiled=True)
+    error_own = (recon_rows.astype(jnp.float32) - target_rows.astype(jnp.float32)) * error_scale
+    error_own = jnp.where(target_rows > 0.5 * vacant_mark, 0.0, error_own).astype(jnp.bfloat16)
+    error_rows = lax.all_gather(error_own, "dp", axis=0, tiled=True)
+    returned = lax.all_to_all(
+        recon_rows.reshape(experts, capacity, features), "expert", split_axis=0, concat_axis=0, tiled=True
     )
-    own_sums = lax.psum_scatter(
-        partials.reshape(leading + (capacity, features)).astype(jnp.bfloat16),
-        "dp",
-        scatter_dimension=row_axis,
-        tiled=True,
-    )
-    recon_rows = own_sums.reshape(experts, capacity, features)
-    returned = lax.all_to_all(recon_rows, "expert", split_axis=0, concat_axis=0, tiled=True)
     recon = lax.dot_general(
         placing,
         returned.reshape(-1, features),
         (((0,), (0,)), ((), ())),
         preferred_element_type=jnp.float32,
     ).astype(jnp.bfloat16)
-    error_tok = ((recon.astype(jnp.float32) - target.astype(jnp.float32)) * error_scale).astype(
-        jnp.bfloat16
-    )
-    error_box = (
-        jnp.dot(placing, error_tok, preferred_element_type=jnp.float32)
-        .astype(jnp.bfloat16)
-        .reshape(experts, capacity, features)
-    )
-    column_errors = lax.all_gather(error_box[:, None], "dp", axis=1, tiled=True)
-    error_in = lax.all_to_all(column_errors, "expert", split_axis=0, concat_axis=0, tiled=True)
-    error_rows = error_in.reshape(-1, features)
     grad_dec = lax.dot_general(
         error_rows, activity, (((0,), (0,)), ((), ())), preferred_element_type=jnp.float32
     ).astype(jnp.bfloat16)

time: 425 us -> 247 us (0.58)
  waiting for transfers between devices: 210 us -> 59.3 us
  local copies, waits for them, and re-layouts: 59.8 us -> 19.2 us
  blocking collectives: 92.4 us -> 110 us
  starting transfers between devices: 7.54 us -> 0.12 us
  other arithmetic: 2.56 us -> 7.69 us
    all_to_all x1 -> x0, waiting for transfers between devices: 63.8 us -> none  [local(): lax.all_to_all(column_rows, 'expert', split_axis=0, concat_axis=0, tiled=...]
    reduce_scatter x1, waiting for transfers between devices: 61.2 us -> 12.2 us  [local(): lax.psum_scatter(partials, 'dp', scatter_dimension=0, tiled=True)]
    all_gather x2, waiting for transfers between devices: 85.4 us -> 47 us  [the longest x1 40.6 us: local(): arrived_rows = lax.all_gather(arrived, 'dp', axis=0, tiled=True)]
    all_to_all x2 -> x3, blocking collectives: 92.4 us -> 110 us  [the longest x1 43.6 us: local(): lax.all_to_all(recon_rows.reshape(experts, capacity, features), 'expert',...]
    all_gather x2 -> x0, local copies, waits for them, and re-layouts: 14.1 us -> none  [the longest x1 8.12 us: local(): column_rows = lax.all_gather(outbox[:, None], 'dp', axis=1, tiled=True)]
    all_to_all x2 -> x0, local copies, waits for them, and re-layouts: 11.9 us -> none  [the longest x1 7.09 us: local(): lax.all_to_all(column_rows, 'expert', split_axis=0, concat_axis=0, tiled=...]
    another operation x4 -> x0, local copies, waits for them, and re-layouts: 10.9 us -> none  [the longest x2 5.47 us: local(): column_errors = lax.all_gather(error_box[:, None], 'dp', axis=1, tiled=True)]
    reshape x3 -> x4, local copies, waits for them, and re-layouts: 17.5 us -> 9.59 us  [the longest x1 2.4 us: local(): recon_rows.reshape(experts, capacity, features)]
  transfers between devices with their start and end apart: 4 -> 3, of which waited for: 4 -> 3; matrix products, arithmetic and copies ran while one was open for 0% -> 8% of each run, Pallas kernels for 0% -> 0%
where the time goes in v1:
time: 247 us; the launch traced here: 246 us
  blocking collectives  110 us (45%)
  waiting for transfers between devices  59.3 us (24%)
  matrix products  36.2 us (15%)
  local copies, waits for them, and re-layouts  19.2 us (8%)
  between operations  13.8 us (6%)
  other arithmetic  7.69 us (3%)
    all_to_all x1, blocking collectives, local(): lax.all_to_all(recon_rows.reshape(experts, capacity, features), 'expert',...  43.6 us
    all_gather x1, waiting for transfers between devices, local(): arrived_rows = lax.all_gather(arrived, 'dp', axis=0, tiled=True)  40.6 us
    all_to_all x1, blocking collectives, local(): lax.all_to_all(target_box.reshape(experts, capacity, features), 'expert',...  34 us
    all_to_all x1, blocking collectives, local(): lax.all_to_all(outbox.reshape(experts, capacity, features), 'expert', spl...  32.3 us
    reduce_scatter x1, waiting for transfers between devices, local(): lax.psum_scatter(partials, 'dp', scatter_dimension=0, tiled=True)  12.2 us
    dot_general x1, matrix products, local(): lax.dot_general(arrived_rows, grad_pre, (((0,), (0,)), ((), ())), preferr...  11.3 us
    dot_general x1, matrix products, local(): lax.dot_general(error_rows, activity, (((0,), (0,)), ((), ())), preferred...  7.27 us
    all_gather x1, waiting for transfers between devices, local(): error_rows = lax.all_gather(error_own, 'dp', axis=0, tiled=True)  6.38 us
  transfers between devices with their start and end apart: 3, of which 3 were waited for; matrix products, arithmetic and copies ran while one was open for 8% of the time, Pallas kernels for 0%

profile of v1, /device:TPU:1, one launch (start us, length us, event | category | flops | bytes accessed | tf_op | source)
XLA Modules:
  0.0 246.2 jit_solution(12084027909192608271)
XLA Ops:
  7.2 0.0 copy-start
  7.2 0.0 all-gather.3.cloned.1.call-start
  7.2 0.9 fusion.11
  8.1 0.2 reduce_window_sum.11
  8.3 0.8 select_reduce_fusion
  9.1 0.7 multiply_add_fusion
  9.8 2.6 %convolution_convert_fusion.3 = bf16[192,3072]{1,0:T(8,128)(2,1)} fusion(bf16[128,3072]{1,0:T(8,128)(2,1)} %param.6, s32[128]{0:T(128)S(1)} %multiply_add_fusion), kind=kOutput, calls=%fused_computation.6 | convolution fusion | flops 151609344 | bytes 1966592 | tf_op jit(solution)/shard_map/dot_general | solution.py:26
  12.4 2.4 reshape.40
  14.8 32.3 %all_to_all.15 = bf16[32,6,3072]{2,1,0:T(8,128)(2,1)} all-to-all(bf16[32,6,3072]{2,1,0:T(8,128)(2,1)} %reshape.40), channel_id=1, replica_groups=mesh['dp'=4,'expert'=32] {'expert'}, dimensions={0} | all-to-all | bytes 2359296 | tf_op jit(solution)/shard_map/all_to_all | solution.py:30
  47.1 0.0 copy-start.2
  47.1 2.4 reshape.41
  49.5 0.0 all-gather.3.cloned.1.call-update
  49.5 0.0 reduce-scatter.2.cloned.1.call-start
  49.6 0.0 copy-done.2
  49.6 40.6 %all-gather.3.cloned.1.call-done = bf16[768,3072]{1,0:T(8,128)(2,1)} async-done(((bf16[192,3072]{1,0:T(8,128)(2,1)}), bf16[768,3072]{1,0:T(8,128)(2,1)}) %all-gather.3.cloned.1.call-update) | async-done | bytes 4718608 | tf_op jit(solution)/shard_map/all_gather | solution.py:36
  90.2 5.4 %fusion.6 = f32[768,512]{1,0:T(8,128)S(1)} fusion(bf16[768,3072]{1,0:T(8,128)(2,1)} %all-gather.3.cloned.1.call-done, bf16[1,3072,512]{2,1,0:T(8,128)(2,1)} %param.10), kind=kOutput, calls=%fused_computation.12 | convolution fusion | flops 2415919104 | bytes 9437184 | tf_op jit(solution)/shard_map/dot_general | solution.py:40
  95.6 0.0 copy-start.3
  95.6 1.2 copy-done.3
  96.8 0.0 copy-done
  96.8 4.5 %convolution_convert_fusion = bf16[768,3072]{1,0:T(8,128)(2,1)} fusion(bf16[1,3072,512]{2,1,0:T(8,128)(2,1)S(1)} %copy-done, f32[768,512]{1,0:T(8,128)S(1)} %fusion.6, f32[512]{0:T(512)S(1)} %bitcast.35), kind=kOutput, calls=%fused_computation | convolution fusion | flops 2421030912 | bytes 9439232 | tf_op jit(solution)/shard_map/dot_general | solution.py:44
  101.3 0.0 reduce-scatter.2.cloned.1.call-update
  101.3 0.0 all-gather.5.cloned.1.call-start
  101.3 0.1 convert_reduce_fusion
  101.5 2.6 %fusion.2 = bf16[192,3072]{1,0:T(8,128)(2,1)} fusion(bf16[128,3072]{1,0:T(8,128)(2,1)} %param.7, f32[192]{0:T(256)S(1)} %subtract_multiply_fusion, s32[128]{0:T(128)S(1)} %multiply_add_fusion), kind=kOutput, calls=%fused_computation.7 | convolution fusion | flops 152199168 | bytes 1967360 | tf_op jit(solution)/shard_map/dot_general | solution.py:28
  104.1 2.4 reshape.44
  106.5 34.0 %all_to_all.16 = bf16[32,6,3072]{2,1,0:T(8,128)(2,1)S(1)} all-to-all(bf16[32,6,3072]{2,1,0:T(8,128)(2,1)} %reshape.44), channel_id=1, replica_groups=mesh['dp'=4,'expert'=32] {'expert'}, dimensions={0} | all-to-all | bytes 2359296 | tf_op jit(solution)/shard_map/all_to_all | solution.py:33
  140.5 0.0 copy-start.1
  140.5 1.1 copy-done.1
  141.6 1.3 broadcast_compare_fusion
  143.0 2.2 gt.11
  145.2 2.7 %reshape.45 = f32[192,3072]{1,0:T(8,128)} reshape(bf16[32,6,3072]{2,1,0:T(8,128)(2,1)} %copy-done.1) | data formatting | bytes 3538944 | tf_op jit(solution)/shard_map/convert_element_type | solution.py:48
  147.8 12.2 %reduce-scatter.2.cloned.1.call-done = bf16[192,3072]{1,0:T(8,128)(2,1)} async-done(((bf16[768,3072]{1,0:T(8,128)(2,1)}), bf16[192,3072]{1,0:T(8,128)(2,1)}) %reduce-scatter.2.cloned.1.call-update) | async-done | bytes 1179664 | tf_op jit(solution)/shard_map/reduce_scatter | solution.py:47
  160.1 3.7 %select_convert_fusion = bf16[192,3072]{1,0:T(8,128)(2,1)} fusion(pred[192,3072]{1,0:T(8,128)(4,1)} %gt.11, f32[192,3072]{1,0:T(8,128)} %reshape.45, bf16[192,3072]{1,0:T(8,128)(2,1)} %reduce-scatter.2.cloned.1.call-done), kind=kLoop, calls=%fused_computation.14 | loop fusion | flops 2949120 | bytes 5308416 | tf_op jit(solution)/shard_map/convert_element_type | solution.py:49
  163.7 0.0 all-gather.5.cloned.1.call-update
  163.8 2.4 reshape.42
  166.2 43.6 %all_to_all.17 = bf16[32,6,3072]{2,1,0:T(8,128)(2,1)} all-to-all(bf16[32,6,3072]{2,1,0:T(8,128)(2,1)} %reshape.42), channel_id=1, replica_groups=mesh['dp'=4,'expert'=32] {'expert'}, dimensions={0} | all-to-all | bytes 2359296 | tf_op jit(solution)/shard_map/all_to_all | solution.py:51
  209.7 2.4 reshape.43
  212.1 2.6 %convolution_convert_fusion.4 = bf16[128,3072]{1,0:T(8,128)(2,1)} fusion(bf16[192,3072]{1,0:T(8,128)(2,1)} %reshape.43, s32[128]{0:T(128)S(1)} %multiply_add_fusion), kind=kOutput, calls=%fused_computation.8 | convolution fusion | flops 151412736 | bytes 1966592 | tf_op jit(solution)/shard_map/dot_general | solution.py:54
  214.7 6.4 %all-gather.5.cloned.1.call-done = bf16[768,3072]{1,0:T(8,128)(2,1)} async-done(((bf16[192,3072]{1,0:T(8,128)(2,1)}), bf16[768,3072]{1,0:T(8,128)(2,1)}) %all-gather.5.cloned.1.call-update) | async-done | bytes 4718608 | tf_op jit(solution)/shard_map/all_gather | solution.py:50
  221.1 11.3 %fusion = bf16[1,3072,512]{2,1,0:T(8,128)(2,1)} fusion(bf16[768,3072]{1,0:T(8,128)(2,1)} %all-gather.3.cloned.1.call-done, bf16[768,3072]{1,0:T(8,128)(2,1)} %all-gather.5.cloned.1.call-done, bf16[1,3072,512]{2,1,0:T(8,128)(2,1)S(1)} %copy-done, f32[768,512]{1,0:T(8,128)} %copy-done.3, f32[512]{0:T(512)S(1)} %bitcast.36), kind=kOutput, calls=%fused_computation.3 | convolution fusion | flops 4837736448 | bytes 17303552 | tf_op jit(solution)/shard_map/dot_general | solution.py:65
  232.4 7.3 %fusion.1 = bf16[1,3072,512]{2,1,0:T(8,128)(2,1)} fusion(bf16[768,3072]{1,0:T(8,128)(2,1)} %all-gather.5.cloned.1.call-done, f32[768,512]{1,0:T(8,128)} %copy-done.3, f32[512]{0:T(512)S(1)} %bitcast.37), kind=kOutput, calls=%fused_computation.4 | convolution fusion | flops 2420244480 | bytes 9439232 | tf_op jit(solution)/shard_map/dot_general | solution.py:60
  (2 shorter events, 0.0 us)
Async XLA Ops:
  7.2 89.6 %copy-start = (bf16[1,3072,512]{2,1,0:T(8,128)(2,1)S(1)}, bf16[1,3072,512]{2,1,0:T(8,128)(2,1)}, u32[]{:S(2)}) copy-start(bf16[1,3072,512]{2,1,0:T(8,128)(2,1)} %param.11) | copy-start | bytes 9437188
  7.2 83.0 %all-gather.3.cloned.1.call-start = ((), (), s32[]{:S(2)}) async-start(), calls=%async_computation.4 | async-start | bytes 5898240 | tf_op jit(solution)/shard_map/all_gather | solution.py:36
  47.1 2.5 %copy-start.2 = (s32[1,512]{1,0:T(1,128)S(1)}, s32[1,512]{1,0:T(1,128)}, u32[]{:S(2)}) copy-start(s32[1,512]{1,0:T(1,128)} %param.9) | copy-start | bytes 6148
  49.5 110.5 %reduce-scatter.2.cloned.1.call-start = ((), (), s32[]{:S(2)}) async-start(), calls=%async_computation.5 | async-start | bytes 5898240 | tf_op jit(solution)/shard_map/reduce_scatter | solution.py:47
  95.6 1.2 copy-start.3
  101.3 119.8 %all-gather.5.cloned.1.call-start = ((), (), s32[]{:S(2)}) async-start(), calls=%async_computation.6 | async-start | bytes 5898240 | tf_op jit(solution)/shard_map/all_gather | solution.py:50
  140.5 1.1 copy-start.1
Sparse Core Ops, SparseCore 0:
  49.6 40.5 all-gather.2
  101.4 58.6 reduce-scatter.1
  163.9 57.1 all-gather.4

commit v2 on v1

v2 whole, which is shorter than its diff:
```python
import functools

import jax
import jax.numpy as jnp
import numpy as np
from jax import lax
from jax.experimental import pallas as pl
from jax.experimental.pallas import tpu as pltpu
from jax.sharding import PartitionSpec as P

MESH = pl.DeviceIdType.MESH
bf16 = jnp.bfloat16
f32 = jnp.float32
error_scale = 0.03125
vacant_mark = 512.0
SLOT = 8
CHUNKS = 4


def slot_table(route_col, experts):
    choices = route_col[:, 0]
    one_hot = (choices[:, None] == jnp.arange(experts, dtype=jnp.int32)[None, :]).astype(jnp.int32)
    ranking = jnp.sum((jnp.cumsum(one_hot, axis=0) - 1) * one_hot, axis=1)
    slot_idx = choices * SLOT + ranking
    positions = jnp.arange(experts * SLOT, dtype=jnp.int32)
    return (positions[:, None] == slot_idx[None, :]).astype(bf16)


def exchange_kernel(
    experts, cap,
    tok_box, tgt_box, shifts_ref, pick_ref, spread_ref, enc_hbm, dec_hbm,
    tokens_out, act_out, err_out, gpre_out, recon_in,
    tok_in, tgt_in, recon_box, tokens, errors, act, deriv, gpre, enc, dec,
    keep, sent_part, got_part, cross_out, cross_in,
    tok_s, tok_r, tgt_s, tgt_r, rec_s, rec_r,
    own_s, own_r, err_s, err_r, part_s, part_r, load_sem, out_sem,
):
    dp = lax.axis_index("dp")
    e = lax.axis_index("expert")
    core = dp % 2
    x = (dp // 2) * 2 + e % 2
    features = tokens.shape[1]
    latents = act.shape[1]
    per = experts // CHUNKS
    rows = per * cap
    span = 4 * rows

    partner = ((dp // 2) * 2 + (dp + 1) % 2, e)
    across = ((dp + 2) % 4, e)

    def odd_dp(turn):
        return ((x + turn + 2 * core) % 4 // 2) * 2 + core

    def dest(k):
        return ((dp if k % 2 == 0 else odd_dp(1)), (e + k) % experts)

    def source(k):
        return ((dp if k % 2 == 0 else odd_dp(3)), (e + experts - k) % experts)

    loads = [
        pltpu.make_async_copy(enc_hbm, enc, load_sem.at[0]),
        pltpu.make_async_copy(dec_hbm, dec, load_sem.at[1]),
    ]
    for load in loads:
        load.start()

    peers = [dest(k) for k in range(1, experts)] + [source(k) for k in range(1, experts, 2)]
    peers += [partner, across]
    barrier = pltpu.get_barrier_semaphore()
    for peer in peers:
        pl.semaphore_signal(barrier, inc=1, device_id=peer, device_id_type=MESH)
    pl.semaphore_wait(barrier, len(peers))

    def remote(src, dst, s, r, to):
        copy = pltpu.make_async_remote_copy(
            src_ref=src, dst_ref=dst, send_sem=s, recv_sem=r, device_id=to, device_id_type=MESH
        )
        copy.start()
        return copy

    tok_copies, tgt_copies = {}, {}
    for box, inbox, s, r, copies in (
        (tok_box, tok_in, tok_s, tok_r, tok_copies),
        (tgt_box, tgt_in, tgt_s, tgt_r, tgt_copies),
    ):
        local = pltpu.make_async_copy(box.at[e], inbox.at[0], r.at[0])
        local.start()
        copies[0] = local
        for k in range(1, experts):
            to = dest(k)
            copies[k] = remote(box.at[to[1]], inbox.at[k], s.at[k], r.at[k], to)

    own, err, part, rec, outs = {}, {}, {}, {}, []

    def share(buf, c, s, r, copies):
        base = c * span
        mine = buf.at[pl.ds(base, rows)]
        copies[c, "across"] = remote(mine, buf.at[pl.ds(base + 2 * rows, rows)], s.at[c, 0], r.at[c, 0], across)
        copies[c, "partner"] = remote(mine, buf.at[pl.ds(base + rows, rows)], s.at[c, 1], r.at[c, 1], partner)

    def relay(buf, c, s, r, copies):
        base = c * span
        copies[c, "across"].wait_recv()
        copies[c, "relay"] = remote(
            buf.at[pl.ds(base + 2 * rows, rows)], buf.at[pl.ds(base + 3 * rows, rows)], s.at[c, 2], r.at[c, 2], partner
        )

    def step_a(c):
        for k in range(c * per, (c + 1) * per):
            if k == 0:
                tok_copies[k].wait()
            else:
                tok_copies[k].wait_recv()
        wide = tok_in[pl.ds(c * per, per)].astype(f32).reshape(per * SLOT, features).astype(bf16)
        tokens[pl.ds(c * span, rows), :] = jnp.dot(
            pick_ref[...], wide, preferred_element_type=f32
        ).astype(bf16)
        share(tokens, c, own_s, own_r, own)

    def step_b(c):
        relay(tokens, c, own_s, own_r, own)

    def step_c(c):
        own[c, "partner"].wait_recv()
        own[c, "relay"].wait_recv()
        base = c * span
        outs.append(pltpu.make_async_copy(tokens.at[pl.ds(base, span)], tokens_out.at[pl.ds(base, span)], out_sem.at[0, c]))
        outs[-1].start()
        if c == 0:
            loads[0].wait()
        tile = 256

        def encode(j, carry):
            cols = pl.ds(pl.multiple_of(j * tile, tile), tile)
            pre = jnp.dot(tokens[pl.ds(base, span), :], enc[:, cols], preferred_element_type=f32) - shifts_ref[:, cols]
            squash = jax.nn.sigmoid(4.0 * pre)
            act[pl.ds(base, span), cols] = (pre * squash).astype(bf16)
            deriv[pl.ds(base, span), cols] = squash + 4.0 * pre * squash * (1.0 - squash)
            return carry

        lax.fori_loop(0, latents // tile, encode, 0)
        outs.append(pltpu.make_async_copy(act.at[pl.ds(base, span)], act_out.at[pl.ds(base, span)], out_sem.at[1, c]))
        outs[-1].start()
        if c == 0:
            loads[1].wait()
        wide = 512

        def decode(j, carry):
            cols = pl.ds(pl.multiple_of(j * wide, wide), wide)
            p = lax.dot_general(
                act[pl.ds(base, span), :], dec[cols, :], (((1,), (1,)), ((), ())), preferred_element_type=f32
            )
            keep[c, 0, :, cols] = p[:rows]
            keep[c, 1, :, cols] = p[2 * rows : 3 * rows]
            sent_part[c, 0, :, cols] = p[rows : 2 * rows].astype(bf16)
            sent_part[c, 1, :, cols] = p[3 * rows :].astype(bf16)
            return carry

        lax.fori_loop(0, features // wide, decode, 0)
        part[c, 1] = remote(sent_part.at[c, 1], got_part.at[c, 1], part_s.at[c, 1], part_r.at[c, 1], partner)
        part[c, 0] = remote(sent_part.at[c, 0], got_part.at[c, 0], part_s.at[c, 0], part_r.at[c, 0], partner)

    def step_d(c):
        part[c, 1].wait_recv()
        cross_out[c] = (keep[c, 1] + got_part[c, 1].astype(f32)).astype(bf16)
        part[c, 2] = remote(cross_out.at[c], cross_in.at[c], part_s.at[c, 2], part_r.at[c, 2], across)

    def step_e(c):
        part[c, 0].wait_recv()
        part[c, 2].wait_recv()
        for k in range(c * per, (c + 1) * per):
            if k == 0:
                tgt_copies[k].wait()
            else:
                tgt_copies[k].wait_recv()
        recon = (keep[c, 0] + got_part[c, 0].astype(f32) + cross_in[c].astype(f32)).astype(bf16)
        wide = tgt_in[pl.ds(c * per, per)].astype(f32).reshape(per * SLOT, features).astype(bf16)
        tgt = jnp.dot(pick_ref[...], wide, preferred_element_type=f32)
        error = (recon.astype(f32) - tgt) * error_scale
        errors[pl.ds(c * span, rows), :] = jnp.where(tgt > 0.5 * vacant_mark, 0.0, error).astype(bf16)
        share(errors, c, err_s, err_r, err)
        padded = jnp.dot(spread_ref[...], recon, preferred_element_type=f32)
        recon_box[pl.ds(c * per, per)] = padded.reshape(per, SLOT, features).astype(bf16)
        for k in range(c * per, (c + 1) * per):
            if k == 0:
                local = pltpu.make_async_copy(recon_box.at[0], recon_in.at[e], rec_r.at[0])
                local.start()
                rec[0] = local
            else:
                rec[k] = remote(recon_box.at[k], recon_in.at[e], rec_s.at[k], rec_r.at[k], source(k))

    def step_f(c):
        relay(errors, c, err_s, err_r, err)

    def step_g(c):
        err[c, "partner"].wait_recv()
        err[c, "relay"].wait_recv()
        base = c * span
        outs.append(pltpu.make_async_copy(errors.at[pl.ds(base, span)], err_out.at[pl.ds(base, span)], out_sem.at[2, c]))
        outs[-1].start()
        tile = 256

        def back(j, carry):
            cols = pl.ds(pl.multiple_of(j * tile, tile), tile)
            grad_act = jnp.dot(errors[pl.ds(base, span), :], dec[:, cols], preferred_element_type=f32)
            gpre[pl.ds(base, span), cols] = (grad_act * deriv[pl.ds(base, span), cols]).astype(bf16)
            return carry

        lax.fori_loop(0, latents // tile, back, 0)
        outs.append(pltpu.make_async_copy(gpre.at[pl.ds(base, span)], gpre_out.at[pl.ds(base, span)], out_sem.at[3, c]))
        outs[-1].start()

    steps = dict(A=step_a, B=step_b, C=step_c, D=step_d, E=step_e, F=step_f, G=step_g)
    order = (
        "A0", "A1", "B0", "A2", "C0", "B1", "A3", "D0", "C1", "B2",
        "D1", "C2", "B3", "D2", "C3", "D3", "E0", "E1", "F0", "E2",
        "F1", "G0", "E3", "F2", "G1", "F3", "G2", "G3",
    )
    for name in order:
        steps[name[0]](int(name[1]))

    for k in range(1, experts):
        tok_copies[k].wait_send()
        tgt_copies[k].wait_send()
        rec[k].wait()
    rec[0].wait()
    for copies in (own, err, part):
        for copy in copies.values():
            copy.wait_send()
    for copy in outs:
        copy.wait()


def exchange(experts, cap, tok_box, tgt_box, shifts, enc, dec):
    features, latents = enc.shape
    per = experts // CHUNKS
    rows = per * cap
    total = 4 * experts * cap
    at = np.arange(rows)
    pick = np.zeros((rows, per * SLOT), np.float32)
    pick[at, at // cap * SLOT + at % cap] = 1.0
    vmem = pl.BlockSpec(memory_space=pltpu.VMEM)
    hbm = pl.BlockSpec(memory_space=pl.ANY)
    dma = pltpu.SemaphoreType.DMA
    box = pltpu.VMEM((experts, SLOT, features), bf16)
    return pl.pallas_call(
        functools.partial(exchange_kernel, experts, cap),
        out_shape=(
            jax.ShapeDtypeStruct((total, features), bf16),
            jax.ShapeDtypeStruct((total, latents), bf16),
            jax.ShapeDtypeStruct((total, features), bf16),
            jax.ShapeDtypeStruct((total, latents), bf16),
            jax.ShapeDtypeStruct((experts, SLOT, features), bf16),
        ),
        in_specs=[vmem] * 5 + [hbm] * 2,
        out_specs=(hbm, hbm, hbm, hbm, vmem),
        scratch_shapes=[
            box, box, box,
            pltpu.VMEM((total, features), bf16),
            pltpu.VMEM((total, features), bf16),
            pltpu.VMEM((total, latents), bf16),
            pltpu.VMEM((total, latents), f32),
            pltpu.VMEM((total, latents), bf16),
            pltpu.VMEM((features, latents), bf16),
            pltpu.VMEM((features, latents), bf16),
            pltpu.VMEM((CHUNKS, 2, rows, features), f32),
            pltpu.VMEM((CHUNKS, 2, rows, features), bf16),
            pltpu.VMEM((CHUNKS, 2, rows, features), bf16),
            pltpu.VMEM((CHUNKS, rows, features), bf16),
            pltpu.VMEM((CHUNKS, rows, features), bf16),
            dma((experts,)), dma((experts,)), dma((experts,)), dma((experts,)), dma((experts,)), dma((experts,)),
            dma((CHUNKS, 3)), dma((CHUNKS, 3)), dma((CHUNKS, 3)), dma((CHUNKS, 3)), dma((CHUNKS, 3)), dma((CHUNKS, 3)),
            dma((2,)), dma((4, CHUNKS)),
        ],
        compiler_params=pltpu.CompilerParams(
            collective_id=0, has_side_effects=True, vmem_limit_bytes=60 * 1024 * 1024
        ),
        name="exchange",
    )(tok_box, tgt_box, shifts, jnp.asarray(pick, bf16), jnp.asarray(pick.T, bf16), enc, dec)


def local(tokens, target, routes, thresholds, enc_weight, dec_weight):
    experts = lax.axis_size("expert")
    per_dev = tokens.shape[0]
    features = tokens.shape[1]
    capacity = 3 * per_dev // (2 * experts)
    placing = slot_table(routes, experts)
    vacant = 1.0 - jnp.sum(placing.astype(f32), axis=1, keepdims=True)
    tok_box = jnp.dot(placing, tokens, preferred_element_type=f32).astype(bf16)
    tgt_box = (jnp.dot(placing, target, preferred_element_type=f32) + vacant * vacant_mark).astype(bf16)
    shape = (experts, SLOT, features)
    shifts = 0.25 * thresholds.astype(f32)
    token_rows, activity, error_rows, grad_pre, returned = exchange(
        experts, capacity, tok_box.reshape(shape), tgt_box.reshape(shape), shifts, enc_weight[0], dec_weight[0]
    )
    recon = lax.dot_general(
        placing, returned.reshape(-1, features), (((0,), (0,)), ((), ())), preferred_element_type=f32
    ).astype(bf16)
    grad_dec = lax.dot_general(
        error_rows, activity, (((0,), (0,)), ((), ())), preferred_element_type=f32
    ).astype(bf16)
    grad_enc = lax.dot_general(
        token_rows, grad_pre, (((0,), (0,)), ((), ())), preferred_element_type=f32
    ).astype(bf16)
    return (recon, grad_enc[None], grad_dec[None])


def solution(mesh):
    in_specs = (
        P(("dp", "expert"), None),
        P(("dp", "expert"), None),
        P(("dp", "expert"), None),
        P("expert", "dp"),
        P("expert", None, "dp"),
        P("expert", None, "dp"),
    )
    out_specs = (P(("dp", "expert"), None), P("expert", None, "dp"), P("expert", None, "dp"))
    return jax.shard_map(local, mesh=mesh, in_specs=in_specs, out_specs=out_specs, check_vma=False)
```

time: 247 us -> 148 us (0.60)
  Pallas kernels: 0 us -> 126 us
  blocking collectives: 110 us -> 0 us
  waiting for transfers between devices: 59.3 us -> 0 us
  local copies, waits for them, and re-layouts: 19.2 us -> 0.03 us
  matrix products: 36.2 us -> 17.3 us
  between operations: 13.8 us -> 0.71 us
  other arithmetic: 7.69 us -> 3.89 us
    pallas_call x0 -> x1, Pallas kernels: none -> 126 us  [exchange(): pl.pallas_call(functools.partial(exchange_kernel, experts, cap), out_shap...]
    all_to_all x3 -> x0, blocking collectives: 110 us -> none  [the longest x1 43.6 us: local(): lax.all_to_all(recon_rows.reshape(experts, capacity, features), 'expert',...]
    all_gather x2 -> x0, waiting for transfers between devices: 47 us -> none  [the longest x1 40.6 us: local(): arrived_rows = lax.all_gather(arrived, 'dp', axis=0, tiled=True)]
    dot_general x5 -> x3, matrix products: 26.4 us -> 10.4 us  [the longest x1 6.97 us: local(): lax.dot_general(token_rows, grad_pre, (((0,), (0,)), ((), ())), preferred...]
    reduce_scatter x1 -> x0, waiting for transfers between devices: 12.2 us -> none  [local(): lax.psum_scatter(partials, 'dp', scatter_dimension=0, tiled=True)]
    reshape x5 -> x0, local copies, waits for them, and re-layouts: 12 us -> none  [the longest x1 2.43 us: local(): returned.reshape(-1, features)]
    convert_element_type x1 -> x0, other arithmetic: 3.68 us -> none  [local(): jnp.where(target_rows > 0.5 * vacant_mark, 0.0, error_own)]
    dot_general x1, matrix products: 7.27 us -> 4.03 us  [local(): lax.dot_general(error_rows, activity, (((0,), (0,)), ((), ())), preferred...]
  transfers between devices with their start and end apart: 3 -> 0, of which waited for: 3 -> 0; matrix products, arithmetic and copies ran while one was open for 8% -> 0% of each run, Pallas kernels for 0% -> 0%
where the time goes in v2:
time: 148 us; the launch traced here: 147 us
  Pallas kernels  126 us (85%)
  matrix products  17.3 us (12%)
  other arithmetic  3.89 us (3%)
    pallas_call x1, Pallas kernels, exchange(): pl.pallas_call(functools.partial(exchange_kernel, experts, cap), out_shap...  126 us
    dot_general x1, matrix products, local(): lax.dot_general(token_rows, grad_pre, (((0,), (0,)), ((), ())), preferred...  6.97 us
    dot_general x1, matrix products, local(): lax.dot_general(error_rows, activity, (((0,), (0,)), ((), ())), preferred...  4.03 us

profile of v2, /device:TPU:1, one launch (start us, length us, event | category | flops | bytes accessed | tf_op | source)
XLA Modules:
  0.0 147.4 jit_solution(3805470762408406681)
XLA Ops:
  0.6 0.0 copy-start
  0.6 0.0 copy-start.1
  0.7 1.4 convert_multiply_fusion.shifts_ref
  2.0 0.7 fusion.10
  2.8 0.2 reduce_window_sum.11
  2.9 0.8 select_reduce_fusion
  3.8 0.7 multiply_add_fusion
  4.4 0.1 convert_reduce_fusion
  4.6 0.0 copy-done
  4.6 1.7 %fusion.4.tgt_box = bf16[32,8,3072]{2,1,0:T(8,128)(2,1)} fusion(bf16[128,3072]{1,0:T(8,128)(2,1)S(1)} %copy-done, f32[256]{0:T(256)S(1)} %subtract_multiply_fusion, s32[128]{0:T(128)S(1)} %multiply_add_fusion), kind=kOutput, calls=%fused_computation.8 | convolution fusion | flops 202932224 | bytes 2360832 | tf_op jit(solution)/shard_map/dot_general | solution.py:290
  6.3 0.0 copy-done.1
  6.3 1.7 %fusion.3.tok_box = bf16[32,8,3072]{2,1,0:T(8,128)(2,1)} fusion(bf16[128,3072]{1,0:T(8,128)(2,1)S(1)} %copy-done.1, s32[128]{0:T(128)S(1)} %multiply_add_fusion), kind=kOutput, calls=%fused_computation.7 | convolution fusion | flops 202145792 | bytes 2359808 | tf_op jit(solution)/shard_map/dot_general | solution.py:289
  8.0 125.5 %exchange.1 = (bf16[768,3072]{1,0:T(8,128)(2,1)}, bf16[768,512]{1,0:T(8,128)(2,1)}, bf16[768,3072]{1,0:T(8,128)(2,1)}, bf16[768,512]{1,0:T(8,128)(2,1)}, bf16[32,8,3072]{2,1,0:T(8,128)(2,1)}) custom-call(bf16[32,8,3072]{2,1,0:T(8,128)(2,1)} %fusion.3.tok_box, bf16[32,8,3072]{2,1,0:T(8,128)(2,1)} %fusion.4.tgt_box, f32[1,512]{1,0:T(1,128)} %convert_multiply_fusion.shifts_ref, ...), custom_call_target="tpu_custom_call" | custom-call | tf_op jit(solution)/shard_map/exchange/pallas_call | solution.py:246
  133.5 0.0 slice-start
  133.5 2.9 %convolution_convert_fusion.3 = bf16[128,3072]{1,0:T(8,128)(2,1)} fusion(bf16[32,8,3072]{2,1,0:T(8,128)(2,1)} %get-tuple-element.8, s32[128]{0:T(128)S(1)} %multiply_add_fusion), kind=kOutput, calls=%fused_computation.9 | convolution fusion | flops 201752576 | bytes 2359808 | tf_op jit(solution)/shard_map/dot_general | solution.py:296
  136.4 0.0 slice-start.1
  136.4 0.0 copy-start.2
  136.4 7.0 %fusion = bf16[1,3072,512]{2,1,0:T(8,128)(2,1)} fusion(bf16[768,3072]{1,0:T(8,128)(2,1)} %get-tuple-element.9, bf16[768,512]{1,0:T(8,128)(2,1)} %get-tuple-element.10), kind=kOutput, calls=%fused_computation.2 | convolution fusion | flops 2417491968 | bytes 8650752 | tf_op jit(solution)/shard_map/dot_general | solution.py:302
  143.4 0.0 slice-done
  143.4 0.0 slice-done.1
  143.4 0.0 copy-done.2
  143.4 4.0 %fusion.1 = bf16[1,3072,512]{2,1,0:T(8,128)(2,1)} fusion(bf16[768,3072]{1,0:T(8,128)(2,1)S(1)} %bitcast.26, bf16[768,512]{1,0:T(8,128)(2,1)S(1)} %copy-done.2), kind=kOutput, calls=%fused_computation.3 | convolution fusion | flops 2417491968 | bytes 8650752 | tf_op jit(solution)/shard_map/dot_general | solution.py:299
  (2 shorter events, 0.0 us)
Async XLA Ops:
  0.6 3.9 %copy-start = (bf16[128,3072]{1,0:T(8,128)(2,1)S(1)}, bf16[128,3072]{1,0:T(8,128)(2,1)}, u32[]{:S(2)}) copy-start(bf16[128,3072]{1,0:T(8,128)(2,1)} %param.9) | copy-start | bytes 2359300
  0.6 5.6 %copy-start.1 = (bf16[128,3072]{1,0:T(8,128)(2,1)S(1)}, bf16[128,3072]{1,0:T(8,128)(2,1)}, u32[]{:S(2)}) copy-start(bf16[128,3072]{1,0:T(8,128)(2,1)} %param.8) | copy-start | bytes 2359300
  133.5 9.9 %slice-start = ((s8[4718592]{0:T(1024)(128)(4,1)}), s8[4194304]{0:T(1024)(128)(4,1)S(1)}, s32[]{:S(2)}) async-start(s8[4718592]{0:T(1024)(128)(4,1)} %bitcast.25), calls=%async_computation | async-start | bytes 8388608
  136.4 7.0 %slice-start.1 = ((s8[4718592]{0:T(1024)(128)(4,1)}), s8[524288]{0:T(1024)(128)(4,1)S(1)}, s32[]{:S(2)}) async-start(s8[4718592]{0:T(1024)(128)(4,1)} %bitcast.25), calls=%async_computation.1 | async-start | bytes 1048576
  136.4 7.0 %copy-start.2 = (bf16[768,512]{1,0:T(8,128)(2,1)S(1)}, bf16[768,512]{1,0:T(8,128)(2,1)}, u32[]{:S(2)}) copy-start(bf16[768,512]{1,0:T(8,128)(2,1)} %get-tuple-element.12) | copy-start | bytes 2359300
